TPU v7x, 32 devices: a whole 2x2x4 slice. The times are simulated.
32 devices in a mesh: seq: 8 (over z, y), mp: 4 (over x, core).
Axes of the slice: x: 2, y: 2, z: 4, core: 2. Of those that a mesh axis runs over, the one named last changes fastest.
Arguments:
- incoming_image_patches: bfloat16 [1, 128, 128, 1152], P(None, 'seq', 'mp'), may hold values from -6 to 6
- initial_standardize_scaling: float32 [1152], replicated, may hold values from 0.1 to 1.9
- acceptance_matrix: bfloat16 [1152, 1024], P(None, 'mp'), may hold values from -0.1875 to 0.1875
- addressing_matrix: bfloat16 [1152, 1024], P(None, 'mp'), may hold values from -0.1875 to 0.1875
- content_matrix: bfloat16 [1152, 1024], P(None, 'mp'), may hold values from -0.1875 to 0.1875
- forgetting_lowdim_left_factor: bfloat16 [1152, 64], replicated, may hold values from -0.1875 to 0.1875
- forgetting_lowdim_right_factor: bfloat16 [64, 1024], P(None, 'mp'), may hold values from -1.5 to 1.5
- forgetting_baseline: float32 [1024], P('mp'), may hold values from -6 to 1
- self_token_reward: float32 [1024], P('mp'), may hold values from -3 to 3
- horizontal_cluster_scaling: float32 [1024], P('mp'), may hold values from 0.1 to 1.9
- vertical_cluster_scaling: float32 [1024], P('mp'), may hold values from 0.1 to 1.9
- temporal_mix_projection_matrix: bfloat16 [1024, 1152], P('mp'), may hold values from -0.1875 to 0.1875
- later_standardize_scaling: float32 [1152], replicated, may hold values from 0.1 to 1.9
- feature_mix_addressing_matrix: bfloat16 [1152, 4608], P('seq', 'mp'), may hold values from -0.1875 to 0.1875
- feature_mix_content_matrix: bfloat16 [4608, 1152], P('mp', 'seq'), may hold values from -0.09375 to 0.09375
Outputs:
- block_out: bfloat16 [1, 128, 128, 1152], P(None, 'seq', 'mp')
All inputs are finite; a program needn't handle non-finite values.
Results may differ from a plain program's by a relative error of at most 0.017.
Values may be sent and summed in bfloat16 or wider, within the bound.
A program may use at most 128 MiB of HBM per device.

v0:
```python
import jax
import jax.numpy as jnp
from jax import lax
from jax.sharding import PartitionSpec as P

SUBSPACE_SIZE = 64


def layer_norm(inputs, gain):
    values = inputs.astype(jnp.float32)
    average = jnp.mean(values, axis=-1, keepdims=True)
    centred = values - average
    spread = jnp.mean(centred * centred, axis=-1, keepdims=True)
    return (centred * lax.rsqrt(spread + 1e-05) * gain).astype(jnp.bfloat16)


def heads_first(array, nheads):
    number, length, inner_width = array.shape
    shaped = array.astype(jnp.float32).reshape(number, length, nheads, inner_width // nheads)
    return shaped.transpose(0, 2, 1, 3)


def recurrence(recept_in, keying_in, decays_in, valued_in, boost_in, gain):
    number, length, inner_width = recept_in.shape
    nheads = inner_width // SUBSPACE_SIZE
    head_size = inner_width // nheads
    blocks = length // 16
    acceptance_horizontal_lines = heads_first(recept_in, nheads)
    addressing_horizontal_lines = heads_first(keying_in, nheads)
    decays = heads_first(decays_in, nheads)
    content_horizontal_lines = heads_first(valued_in, nheads)
    boost = boost_in.reshape(nheads, 1, head_size)
    running = jnp.cumsum(decays, axis=2)
    before = running - decays
    before_blocks = before.reshape(number, nheads, blocks, 16, head_size)
    anchor = before_blocks[:, :, :, :1, :]
    queries = acceptance_horizontal_lines.reshape(number, nheads, blocks, 16, head_size) * jnp.exp(
        before_blocks - anchor
    )
    places = jnp.arange(length)
    limits = (jnp.arange(blocks) + 1) * 16
    usable = places[None, :] < limits[:, None]
    exponent = anchor - running[:, :, None, :, :]
    exponent = jnp.where(usable[None, None, :, :, None], exponent, -10000.0)
    weighted = addressing_horizontal_lines[:, :, None, :, :] * jnp.exp(exponent)
    scores = jnp.einsum("nhbqc,nhbsc->nhbqs", queries, weighted, precision=lax.Precision.HIGHEST)
    query_places = places.reshape(blocks, 16)
    earlier = places[None, None, :] < query_places[:, :, None]
    scores = jnp.where(earlier[None, None], scores, 0.0)
    current = jnp.sum(acceptance_horizontal_lines * boost * addressing_horizontal_lines, axis=-1)
    summed = jnp.einsum(
        "nhbqs,nhsc->nhbqc", scores, content_horizontal_lines, precision=lax.Precision.HIGHEST
    )
    summed = (
        summed.reshape(number, nheads, length, head_size)
        + current[..., None] * content_horizontal_lines
    )
    average = jnp.mean(summed, axis=-1, keepdims=True)
    centred = summed - average
    spread = jnp.mean(centred * centred, axis=-1, keepdims=True)
    normed = (
        (centred * lax.rsqrt(spread + 0.00064))
        .transpose(0, 2, 1, 3)
        .reshape(number, length, inner_width)
    )
    return (normed * gain).astype(jnp.bfloat16)


def lines_of_columns(array):
    images, height, columns, inner_width = array.shape
    return jnp.swapaxes(array, 1, 2).reshape(images * columns, height, inner_width)


def shards(
    incoming_image_patches,
    initial_standardize_scaling,
    acceptance_matrix,
    addressing_matrix,
    content_matrix,
    forgetting_lowdim_left_factor,
    forgetting_lowdim_right_factor,
    forgetting_baseline,
    self_token_reward,
    horizontal_cluster_scaling,
    vertical_cluster_scaling,
    temporal_mix_projection_matrix,
    later_standardize_scaling,
    feature_mix_addressing_matrix,
    feature_mix_content_matrix,
):
    images, row_count, part_cols, model_width = incoming_image_patches.shape
    whole_rows = lax.all_gather(incoming_image_patches, "mp", axis=2, tiled=True)
    full_cols = whole_rows.shape[2]
    inner_width = acceptance_matrix.shape[1]
    grid_shape = (images, row_count, full_cols, inner_width)
    xn1 = layer_norm(whole_rows, initial_standardize_scaling).reshape(-1, model_width)
    acceptance_horizontal_lines = jnp.dot(
        xn1, acceptance_matrix, preferred_element_type=jnp.float32
    ).astype(jnp.bfloat16)
    addressing_horizontal_lines = jnp.dot(
        xn1, addressing_matrix, preferred_element_type=jnp.float32
    ).astype(jnp.bfloat16)
    content_horizontal_lines = jnp.dot(
        xn1, content_matrix, preferred_element_type=jnp.float32
    ).astype(jnp.bfloat16)
    latent = jnp.tanh(
        jnp.dot(xn1, forgetting_lowdim_left_factor, preferred_element_type=jnp.float32)
    ).astype(jnp.bfloat16)
    forgetting_log_amount = (
        -0.7
        * jax.nn.sigmoid(
            forgetting_baseline
            + jnp.dot(latent, forgetting_lowdim_right_factor, preferred_element_type=jnp.float32)
        )
    ).astype(jnp.bfloat16)
    recept_grid = acceptance_horizontal_lines.reshape(grid_shape)
    keying_grid = addressing_horizontal_lines.reshape(grid_shape)
    decay_grid = forgetting_log_amount.reshape(grid_shape)
    line_shape = (images * row_count, full_cols, inner_width)
    horizontal_recurrence_result = recurrence(
        acceptance_horizontal_lines.reshape(line_shape),
        addressing_horizontal_lines.reshape(line_shape),
        forgetting_log_amount.reshape(line_shape),
        content_horizontal_lines.reshape(line_shape),
        self_token_reward,
        horizontal_cluster_scaling,
    )
    col_recept, col_keying, col_decay, col_valued = (
        lax.all_to_all(recept_grid, "seq", split_axis=2, concat_axis=1, tiled=True),
        lax.all_to_all(keying_grid, "seq", split_axis=2, concat_axis=1, tiled=True),
        lax.all_to_all(decay_grid, "seq", split_axis=2, concat_axis=1, tiled=True),
        lax.all_to_all(
            horizontal_recurrence_result.reshape(grid_shape),
            "seq",
            split_axis=2,
            concat_axis=1,
            tiled=True,
        ),
    )
    height = col_recept.shape[1]
    columns = col_recept.shape[2]
    vertical_recurrence_result = recurrence(
        lines_of_columns(col_recept),
        lines_of_columns(col_keying),
        lines_of_columns(col_decay),
        lines_of_columns(col_valued),
        self_token_reward,
        vertical_cluster_scaling,
    )
    back_grid = jnp.swapaxes(
        vertical_recurrence_result.reshape(images, columns, height, inner_width), 1, 2
    )
    row_grid = lax.all_to_all(back_grid, "seq", split_axis=1, concat_axis=2, tiled=True)
    partial_value = jnp.dot(
        row_grid.reshape(-1, inner_width),
        temporal_mix_projection_matrix,
        preferred_element_type=jnp.float32,
    )
    partial_value = lax.optimization_barrier(partial_value.astype(jnp.bfloat16)).astype(jnp.float32)
    partial_value = partial_value.reshape(images, row_count, full_cols, model_width)
    totals = lax.psum(partial_value.astype(jnp.bfloat16), "mp").astype(jnp.float32)
    residual_all = (whole_rows.astype(jnp.float32) + totals).astype(jnp.bfloat16)
    mix_input = layer_norm(residual_all, later_standardize_scaling)
    residual = lax.dynamic_slice_in_dim(
        residual_all, lax.axis_index("mp") * part_cols, part_cols, 2
    )
    flattened = mix_input.reshape(-1, model_width)
    hidden_pre = jnp.dot(
        flattened,
        lax.all_gather(feature_mix_addressing_matrix, "seq", axis=0, tiled=True),
        preferred_element_type=jnp.float32,
    )
    positive = jnp.maximum(hidden_pre, 0.0)
    hidden = (positive * positive).astype(jnp.bfloat16)
    downward = jnp.dot(
        hidden,
        lax.all_gather(feature_mix_content_matrix, "seq", axis=1, tiled=True),
        preferred_element_type=jnp.float32,
    )
    downward = lax.optimization_barrier(downward.astype(jnp.bfloat16)).astype(jnp.float32)
    downward = downward.reshape(images, row_count, full_cols, model_width)
    mixed = lax.psum_scatter(
        downward.astype(jnp.bfloat16), "mp", scatter_dimension=2, tiled=True
    ).astype(jnp.float32)
    return (residual.astype(jnp.float32) + mixed).astype(jnp.bfloat16)


def solution(mesh):
    placed = (
        P(None, "seq", "mp", None),
        P(),
        P(None, "mp"),
        P(None, "mp"),
        P(None, "mp"),
        P(),
        P(None, "mp"),
        P("mp"),
        P("mp"),
        P("mp"),
        P("mp"),
        P("mp", None),
        P(),
        P("seq", "mp"),
        P("mp", "seq"),
    )
    return jax.shard_map(
        shards, mesh=mesh, in_specs=placed, out_specs=P(None, "seq", "mp", None), check_vma=False
    )
```

profile of v0, /device:TPU:0, one launch (start us, length us, event | category | flops | bytes accessed | tf_op | source)
XLA Modules:
  0.0 550.7 jit_solution(13070111403937969308)
XLA Ops:
  9.0 40.9 %all-gather.4.cloned.1.call-done = bf16[1,16,128,1152]{3,2,1,0:T(8,128)(2,1)} async-done(((bf16[1,16,32,1152]{3,2,1,0:T(8,128)(2,1)}), bf16[1,16,128,1152]{3,2,1,0:T(8,128)(2,1)}) %all-gather.4.cloned.1.call-update) | async-done | bytes 4718608 | tf_op jit(solution)/shard_map/all_gather | solution.py:92
  63.9 4.9 copy.216
  68.8 4.8 copy.187
  73.7 4.5 fusion.54
  81.3 8.0 %bitcast_subtract_fusion = (f32[16,4,128,64]{3,0,1,2:T(8,128)S(1)}, f32[16,4,128,64]{3,0,1,2:T(8,128)}) fusion(f32[16,128,4,64]{3,2,1,0:T(4,128)} %reshape.302), kind=kOutput, calls=%fused_computation.42 | output fusion | flops 67108864 | bytes 6291456 | tf_op jit(solution)/shard_map/jit(cumsum)/reduce_window_sum | solution.py:33
  91.4 4.8 copy.196
  108.3 5.7 %convolution_convert_fusion.2 = bf16[2048,256]{1,0:T(8,128)(2,1)} fusion(bf16[2048,1152]{1,0:T(8,128)(2,1)} %bitcast.152, bf16[1152,256]{1,0:T(8,128)(2,1)} %param.19), kind=kOutput, calls=%fused_computation.66 | convolution fusion | flops 1208483840 | bytes 6356992 | tf_op jit(solution)/shard_map/dot_general | solution.py:103
  117.8 22.1 %fusion.1 = f32[16,4,8,16,128]{4,3,2,1,0:T(8,128)S(1)} fusion(f32[16,4,128,64]{2,3,1,0:T(8,128)} %copy.196, f32[16,4,8,64]{3,2,1,0:T(8,128)S(1)} %copy.191, f32[16,4,128,64]{2,3,1,0:T(8,128)S(1)} %bitcast.135, pred[8,128]{1,0:T(8,128)(4,1)S(1)} %iota_compare_fusion.1, f32[16,4,8,16,64]{4,3,2,1,0:T(8,128)} %bitcast.161, f32[16,4,8,16,64]{4,0,1,3,2:T(8,128)} %bitcast.147), kind=kOutput, calls=%fused_computation.1 | convolution fusion | flops 818937856 | bytes 12715008 | tf_op jit(solution)/shard_map/nhbqc,nhbsc->nhbqs/dot_general | solution.py:46
  156.3 5.6 %all-to-all-start.3 = ((bf16[1,16,128,256]{3,1,0,2:T(8,128)(2,1)}), bf16[1,16,128,256]{3,1,0,2:T(8,128)(2,1)}, u32[]{:S(2)}, u32[]{:S(2)}) async-start(bf16[1,16,128,256]{3,1,0,2:T(8,128)(2,1)} %multiply_convert_fusion.1), calls=%async_computation.3 | async-start | bytes 2097152 | tf_op jit(solution)/shard_map/all_to_all | solution.py:132
  164.8 23.4 %all-to-all-done.3 = bf16[1,16,128,256]{3,1,0,2:T(8,128)(2,1)} async-done(((bf16[1,16,128,256]{3,1,0,2:T(8,128)(2,1)}), bf16[1,16,128,256]{3,1,0,2:T(8,128)(2,1)}, u32[]{:S(2)}, u32[]{:S(2)}) %all-to-all-start.3) | async-done | bytes 1048608 | tf_op jit(solution)/shard_map/all_to_all | solution.py:132
  188.2 4.2 all-to-all-start.1
  194.0 24.0 %all-to-all-done.1 = bf16[1,16,128,256]{3,1,0,2:T(8,128)(2,1)} async-done(((bf16[1,16,128,256]{3,1,0,2:T(8,128)(2,1)}), bf16[1,16,128,256]{3,1,0,2:T(8,128)(2,1)}, u32[]{:S(2)}, u32[]{:S(2)}) %all-to-all-start.1) | async-done | bytes 1048608 | tf_op jit(solution)/shard_map/all_to_all | solution.py:131
  223.2 24.2 %all-to-all-done = bf16[1,16,128,256]{3,1,0,2:T(8,128)(2,1)S(1)} async-done(((bf16[1,16,128,256]{3,1,0,2:T(8,128)(2,1)}), bf16[1,16,128,256]{3,1,0,2:T(8,128)(2,1)S(1)}, u32[]{:S(2)}, u32[]{:S(2)}) %all-to-all-start) | async-done | bytes 1048608 | tf_op jit(solution)/shard_map/all_to_all | solution.py:129
  247.5 4.2 all-to-all-start.2
  260.5 4.6 copy.177
  265.1 6.1 %bitcast_subtract_fusion.1 = (f32[16,4,128,64]{3,0,1,2:T(8,128)S(1)}, f32[16,4,128,64]{3,0,1,2:T(8,128)}) fusion(f32[16,128,4,64]{3,0,2,1:T(8,128)} %copy.177), kind=kOutput, calls=%fused_computation.45 | output fusion | flops 67108864 | bytes 6291456 | tf_op jit(solution)/shard_map/jit(cumsum)/reduce_window_sum | solution.py:33
  273.4 4.7 copy.185
  291.5 22.4 %fusion.6 = f32[16,4,8,16,128]{4,3,2,1,0:T(8,128)S(1)} fusion(f32[16,4,128,64]{2,3,1,0:T(8,128)} %copy.185, f32[16,4,8,64]{3,2,1,0:T(8,128)S(1)} %copy.178, f32[16,4,128,64]{2,3,1,0:T(8,128)} %bitcast.140, pred[8,128]{1,0:T(8,128)(4,1)S(1)} %iota_compare_fusion.1, f32[16,4,8,16,64]{4,3,2,1,0:T(8,128)} %bitcast.160, f32[16,4,8,16,64]{4,0,1,3,2:T(8,128)} %bitcast.145), kind=kOutput, calls=%fused_computation.6 | convolution fusion | flops 818937856 | bytes 12715008 | tf_op jit(solution)/shard_map/nhbqc,nhbsc->nhbqs/dot_general | solution.py:46
  330.0 30.6 %all_to_all.69 = bf16[1,128,16,256]{3,2,0,1:T(8,128)(2,1)S(1)} all-to-all(bf16[1,128,16,256]{3,2,0,1:T(8,128)(2,1)S(1)} %fusion.68), channel_id=1, replica_groups=mesh['seq'=8,'mp'=4] {'seq'}, dimensions={1} | all-to-all | bytes 2097152 | tf_op jit(solution)/shard_map/all_to_all | solution.py:153
  365.7 91.0 %all-reduce.2.cloned.1.call-done = bf16[1,16,128,1152]{3,2,1,0:T(8,128)(2,1)} async-done(((bf16[1,16,128,1152]{3,2,1,0:T(8,128)(2,1)}), bf16[1,16,128,1152]{3,2,1,0:T(8,128)(2,1)}) %all-reduce.2.cloned.1.call-update) | async-done | bytes 4718608 | tf_op jit(solution)/shard_map/psum | solution.py:161
  456.6 5.3 convert_reduce_fusion.1
  467.3 8.3 %all-gather.8.cloned.1.call-done = bf16[1152,1152]{0,1:T(8,128)(2,1)} async-done(((bf16[1152,144]{0,1:T(8,128)(2,1)}), bf16[1152,1152]{0,1:T(8,128)(2,1)}) %all-gather.8.cloned.1.call-update) | async-done | bytes 2654224 | tf_op jit(solution)/shard_map/all_gather | solution.py:177
  475.5 18.4 %convolution_convert_fusion = bf16[2048,1152]{1,0:T(8,128)(2,1)} fusion(bf16[1152,1152]{0,1:T(8,128)(2,1)} %all-gather.8.cloned.1.call-done, bf16[2048,1152]{1,0:T(8,128)(2,1)} %bitcast.153, bf16[1152,1152]{1,0:T(8,128)(2,1)} %all-gather.6.cloned.1.call-done), kind=kOutput, calls=%fused_computation.40 | convolution fusion | flops 10881073152 | bytes 14745600 | tf_op jit(solution)/shard_map/dot_general | solution.py:175
  493.9 46.6 %reduce-scatter.2.cloned.1.call-done = bf16[1,16,32,1152]{3,2,1,0:T(8,128)(2,1)} async-done(((bf16[1,16,128,1152]{3,2,1,0:T(8,128)(2,1)}), bf16[1,16,32,1152]{3,2,1,0:T(8,128)(2,1)}) %reduce-scatter.2.cloned.1.call-update) | async-done | bytes 1179664 | tf_op jit(solution)/shard_map/reduce_scatter | solution.py:182
  (135 shorter events, 116.1 us)
Async XLA Ops:
  7.4 353.3 %copy-start = (bf16[256,1152]{1,0:T(8,128)(2,1)S(1)}, bf16[256,1152]{1,0:T(8,128)(2,1)}, u32[]{:S(2)}) copy-start(bf16[256,1152]{1,0:T(8,128)(2,1)} %param.26) | copy-start | bytes 1769476
  7.4 42.5 %all-gather.4.cloned.1.call-start = ((), (), s32[]{:S(2)}) async-start(), calls=%async_computation.6 | async-start | bytes 5898240 | tf_op jit(solution)/shard_map/all_gather | solution.py:92
  9.0 46.1 %copy-start.17 = (f32[1152]{0:T(1024)S(1)}, f32[1152]{0:T(1024)}, u32[]{:S(2)}) copy-start(f32[1152]{0:T(1024)} %param.16) | copy-start | bytes 13828
  60.8 8.0 %copy-start.10 = (bf16[2048,256]{1,0:T(8,128)(2,1)}, bf16[2048,256]{1,0:T(8,128)(2,1)S(1)}, u32[]{:S(2)}) copy-start(bf16[2048,256]{1,0:T(8,128)(2,1)S(1)} %convolution_convert_fusion.4) | copy-start | bytes 3145732
  68.8 4.8 copy-start.23
  68.8 4.8 copy-start.24
  68.8 4.8 copy-start.25
  78.1 11.1 %copy-start.14 = (bf16[2048,256]{1,0:T(8,128)(2,1)}, bf16[2048,256]{1,0:T(8,128)(2,1)S(1)}, u32[]{:S(2)}) copy-start(bf16[2048,256]{1,0:T(8,128)(2,1)S(1)} %fusion.54) | copy-start | bytes 3145732
  89.3 7.0 %copy-start.22 = (bf16[1152,256]{1,0:T(8,128)(2,1)S(1)}, bf16[1152,256]{1,0:T(8,128)(2,1)}, u32[]{:S(2)}) copy-start(bf16[1152,256]{1,0:T(8,128)(2,1)} %param.18) | copy-start | bytes 1769476
  108.3 9.5 %copy-start.6 = (f32[16,128,4,64]{1,3,2,0:T(8,128)}, f32[16,128,4,64]{1,3,2,0:T(8,128)S(1)}, u32[]{:S(2)}) copy-start(f32[16,128,4,64]{1,3,2,0:T(8,128)S(1)} %copy.194) | copy-start | bytes 6291460
  117.8 22.1 %copy-start.3 = (bf16[32,8,16,128]{3,2,1,0:T(8,128)(2,1)}, bf16[32,8,16,128]{3,2,1,0:T(8,128)(2,1)S(1)}, u32[]{:S(2)}) copy-start(bf16[32,8,16,128]{3,2,1,0:T(8,128)(2,1)S(1)} %copy.223) | copy-start | bytes 3145732
  156.3 36.2 %copy-start.11 = (bf16[2048,256]{1,0:T(8,128)(2,1)S(1)}, bf16[2048,256]{1,0:T(8,128)(2,1)}, u32[]{:S(2)}) copy-start(bf16[2048,256]{1,0:T(8,128)(2,1)} %copy-done.10) | copy-start | bytes 3145732
  156.3 31.9 %all-to-all-start.3 = ((bf16[1,16,128,256]{3,1,0,2:T(8,128)(2,1)}), bf16[1,16,128,256]{3,1,0,2:T(8,128)(2,1)}, u32[]{:S(2)}, u32[]{:S(2)}) async-start(bf16[1,16,128,256]{3,1,0,2:T(8,128)(2,1)} %multiply_convert_fusion.1), calls=%async_computation.3 | async-start | bytes 2097152 | tf_op jit(solution)/shard_map/all_to_all | solution.py:132
  161.9 59.7 %copy-start.13 = (bf16[2048,256]{1,0:T(8,128)(2,1)S(1)}, bf16[2048,256]{1,0:T(8,128)(2,1)}, u32[]{:S(2)}) copy-start(bf16[2048,256]{1,0:T(8,128)(2,1)} %copy-done.12) | copy-start | bytes 3145732
  188.2 29.8 %all-to-all-start.1 = ((bf16[1,16,128,256]{3,1,0,2:T(8,128)(2,1)}), bf16[1,16,128,256]{3,1,0,2:T(8,128)(2,1)}, u32[]{:S(2)}, u32[]{:S(2)}) async-start(bf16[1,16,128,256]{3,1,0,2:T(8,128)(2,1)} %copy.173), calls=%async_computation.1 | async-start | bytes 2097152 | tf_op jit(solution)/shard_map/all_to_all | solution.py:131
  218.1 29.4 %all-to-all-start = ((bf16[1,16,128,256]{3,1,0,2:T(8,128)(2,1)}), bf16[1,16,128,256]{3,1,0,2:T(8,128)(2,1)S(1)}, u32[]{:S(2)}, u32[]{:S(2)}) async-start(bf16[1,16,128,256]{3,1,0,2:T(8,128)(2,1)} %copy.168), calls=%async_computation | async-start | bytes 2097152 | tf_op jit(solution)/shard_map/all_to_all | solution.py:129
  247.5 7.7 %copy-start.15 = (bf16[1,16,128,256]{3,1,0,2:T(8,128)(2,1)}, bf16[1,16,128,256]{3,1,0,2:T(8,128)(2,1)S(1)}, u32[]{:S(2)}) copy-start(bf16[1,16,128,256]{3,1,0,2:T(8,128)(2,1)S(1)} %all-to-all-done) | copy-start | bytes 3145732
  247.5 37.7 %all-to-all-start.2 = ((bf16[1,16,128,256]{3,1,0,2:T(8,128)(2,1)}), bf16[1,16,128,256]{3,1,0,2:T(8,128)(2,1)}, u32[]{:S(2)}, u32[]{:S(2)}) async-start(bf16[1,16,128,256]{3,1,0,2:T(8,128)(2,1)} %copy.180), calls=%async_computation.2 | async-start | bytes 2097152 | tf_op jit(solution)/shard_map/all_to_all | solution.py:130
  251.7 204.9 %all-reduce.2.cloned.1.call-start = ((), (), s32[]{:S(2)}) async-start(), calls=%async_computation.7 | async-start | bytes 9437184 | tf_op jit(solution)/shard_map/psum | solution.py:161
  271.2 7.0 %copy-start.16 = (bf16[1,16,128,256]{3,1,0,2:T(8,128)(2,1)S(1)}, bf16[1,16,128,256]{3,1,0,2:T(8,128)(2,1)}, u32[]{:S(2)}) copy-start(bf16[1,16,128,256]{3,1,0,2:T(8,128)(2,1)} %copy-done.15) | copy-start | bytes 3145732
  291.5 22.4 %copy-start.5 = (bf16[1,16,128,256]{2,3,1,0:T(8,128)(2,1)S(1)}, bf16[1,16,128,256]{2,3,1,0:T(8,128)(2,1)}, u32[]{:S(2)}) copy-start(bf16[1,16,128,256]{2,3,1,0:T(8,128)(2,1)} %copy.204) | copy-start | bytes 3145732
  364.4 102.8 %all-gather.6.cloned.1.call-start = ((), (), s32[]{:S(2)}) async-start(), calls=%async_computation.8 | async-start | bytes 2985984 | tf_op jit(solution)/shard_map/all_gather | solution.py:170
  365.0 110.5 %all-gather.8.cloned.1.call-start = ((), (), s32[]{:S(2)}) async-start(), calls=%async_computation.9 | async-start | bytes 2985984 | tf_op jit(solution)/shard_map/all_gather | solution.py:177
  365.6 174.9 %reduce-scatter.2.cloned.1.call-start = ((), (), s32[]{:S(2)}) async-start(), calls=%async_computation.10 | async-start | bytes 5898240 | tf_op jit(solution)/shard_map/reduce_scatter | solution.py:182
  (11 other events, 28.9 us)
Sparse Core Ops, SparseCore 0:
  9.7 40.1 all-gather.3
  364.6 92.0 all-reduce.1
  494.0 46.4 reduce-scatter.1
Sparse Core Ops, SparseCore 1:
  367.1 52.9 all-gather.5
  422.1 53.4 all-gather.7
where the time goes:
time: 554 us; the launch traced here: 551 us
  waiting for transfers between devices  260 us (47%)
  local copies, waits for them, and re-layouts  89.8 us (16%)
  matrix products  89.8 us (16%)
  other arithmetic  47.2 us (9%)
  blocking collectives  30.6 us (6%)
  starting transfers between devices  17.9 us (3%)
  between operations  15.3 us (3%)
    psum x1, waiting for transfers between devices, shards(): lax.psum(partial_value.astype(jnp.bfloat16), 'mp').astype(jnp.float32)  91 us
    reduce_scatter x1, waiting for transfers between devices, shards(): lax.psum_scatter(downward.astype(jnp.bfloat16), 'mp', scatter_dimension=2...  46.6 us
    dot_general x2, matrix products, recurrence(): jnp.einsum('nhbqc,nhbsc->nhbqs', queries, weighted, precision=lax.Precisi...  44.5 us
    transpose x14, local copies, waits for them, and re-layouts, heads_first(): return shaped.transpose(0, 2, 1, 3)  42.1 us
    all_gather x1, waiting for transfers between devices, shards(): lax.all_gather(incoming_image_patches, 'mp', axis=2, tiled=True)  40.9 us
    all_to_all x1, blocking collectives, shards(): lax.all_to_all(back_grid, 'seq', split_axis=1, concat_axis=2, tiled=True)  30.6 us
    all_to_all x1, waiting for transfers between devices, shards(): lax.all_to_all(recept_grid, 'seq', split_axis=2, concat_axis=1, tiled=True)  24.2 us
    all_to_all x1, waiting for transfers between devices, shards(): lax.all_to_all(decay_grid, 'seq', split_axis=2, concat_axis=1, tiled=True)  24 us
  transfers between devices with their start and end apart: 9, of which 7 were waited for; matrix products, arithmetic and copies ran while one was open for 9% of the time, Pallas kernels for 0%

commit v1 on v0

--- a/solution.py
+++ b/solution.py
@@ -89,7 +89,12 @@
     feature_mix_content_matrix,
 ):
     images, row_count, part_cols, model_width = incoming_image_patches.shape
-    whole_rows = lax.all_gather(incoming_image_patches, "mp", axis=2, tiled=True)
+    ring = [incoming_image_patches]
+    for hop in range(3):
+        ring.append(lax.ppermute(ring[-1], "mp", [(dev, (dev + 1) % 4) for dev in range(4)]))
+    whole_rows = jnp.roll(
+        jnp.concatenate(ring[::-1], axis=2), (lax.axis_index("mp") + 1) * ring[0].shape[2], axis=2
+    )
     full_cols = whole_rows.shape[2]
     inner_width = acceptance_matrix.shape[1]
     grid_shape = (images, row_count, full_cols, inner_width)

time: 554 us -> 564 us (1.018)
    ppermute x0 -> x3, waiting for transfers between devices: none -> 46.8 us  [shards(): lax.ppermute(ring[-1], 'mp', [(dev, (dev + 1) % 4) for dev in range(4)])]
    all_gather x1 -> x0, waiting for transfers between devices: 40.9 us -> none  [shards(): lax.all_gather(incoming_image_patches, 'mp', axis=2, tiled=True)]
    all_to_all x1, waiting for transfers between devices: 24.2 us -> 0.01 us  [shards(): lax.all_to_all(recept_grid, 'seq', split_axis=2, concat_axis=1, tiled=True)]
    all_to_all x1, waiting for transfers between devices: 0.01 us -> 24.2 us  [shards(): lax.all_to_all(keying_grid, 'seq', split_axis=2, concat_axis=1, tiled=True)]
    all_gather x1, waiting for transfers between devices: 8.25 us -> 0.01 us  [shards(): lax.all_gather(feature_mix_content_matrix, 'seq', axis=1, tiled=True)]
    all_gather x1, waiting for transfers between devices: 0.01 us -> 8.25 us  [shards(): lax.all_gather(feature_mix_addressing_matrix, 'seq', axis=0, tiled=True)]
    unnamed x53 -> x58, local copies, waits for them, and re-layouts: 9.93 us -> 13.2 us
  transfers between devices with their start and end apart: 9 -> 11, of which waited for: 7 -> 9; matrix products, arithmetic and copies ran while one was open for 9% -> 8% of each run, Pallas kernels for 0% -> 0%
where the time goes in v1:
time: 564 us; the launch traced here: 559 us
  waiting for transfers between devices  264 us (47%)
  local copies, waits for them, and re-layouts  91.8 us (16%)
  matrix products  90.1 us (16%)
  other arithmetic  47.4 us (8%)
  blocking collectives  30.6 us (5%)
  starting transfers between devices  19.5 us (3%)
  between operations  15.7 us (3%)
    psum x1, waiting for transfers between devices, shards(): lax.psum(partial_value.astype(jnp.bfloat16), 'mp').astype(jnp.float32)  91 us
    ppermute x3, waiting for transfers between devices, shards(): lax.ppermute(ring[-1], 'mp', [(dev, (dev + 1) % 4) for dev in range(4)])  46.8 us
    reduce_scatter x1, waiting for transfers between devices, shards(): lax.psum_scatter(downward.astype(jnp.bfloat16), 'mp', scatter_dimension=2...  46.6 us
    dot_general x2, matrix products, recurrence(): jnp.einsum('nhbqc,nhbsc->nhbqs', queries, weighted, precision=lax.Precisi...  44.7 us
    transpose x14, local copies, waits for them, and re-layouts, heads_first(): return shaped.transpose(0, 2, 1, 3)  38.8 us
    all_to_all x1, blocking collectives, shards(): lax.all_to_all(back_grid, 'seq', split_axis=1, concat_axis=2, tiled=True)  30.6 us
    all_to_all x1, waiting for transfers between devices, shards(): lax.all_to_all(keying_grid, 'seq', split_axis=2, concat_axis=1, tiled=True)  24.2 us
    all_to_all x1, waiting for transfers between devices, shards(): lax.all_to_all(decay_grid, 'seq', split_axis=2, concat_axis=1, tiled=True)  23.8 us
  transfers between devices with their start and end apart: 11, of which 9 were waited for; matrix products, arithmetic and copies ran while one was open for 8% of the time, Pallas kernels for 0%

profile of v1, /device:TPU:0, one launch (start us, length us, event | category | flops | bytes accessed | tf_op | source)
XLA Modules:
  0.0 559.2 jit_solution(9488123631591031810)
XLA Ops:
  7.9 16.0 %collective-permute-done = bf16[1,16,32,1152]{3,2,1,0:T(8,128)(2,1)S(1)} collective-permute-done((bf16[1,16,32,1152]{3,2,1,0:T(8,128)(2,1)}, bf16[1,16,32,1152]{3,2,1,0:T(8,128)(2,1)S(1)}, u32[]{:S(2)}, u32[]{:S(2)}) %collective-permute-start) | collective-permute-done | bytes 1179680 | tf_op jit(solution)/shard_map/ppermute | solution.py:94
  23.9 15.7 %collective-permute-done.1 = bf16[1,16,32,1152]{3,2,1,0:T(8,128)(2,1)} collective-permute-done((bf16[1,16,32,1152]{3,2,1,0:T(8,128)(2,1)S(1)}, bf16[1,16,32,1152]{3,2,1,0:T(8,128)(2,1)}, u32[]{:S(2)}, u32[]{:S(2)}) %collective-permute-start.1) | collective-permute-done | bytes 1179680 | tf_op jit(solution)/shard_map/ppermute | solution.py:94
  40.6 15.0 %collective-permute-done.2 = bf16[1,16,32,1152]{3,2,1,0:T(8,128)(2,1)} collective-permute-done((bf16[1,16,32,1152]{3,2,1,0:T(8,128)(2,1)}, bf16[1,16,32,1152]{3,2,1,0:T(8,128)(2,1)}, u32[]{:S(2)}, u32[]{:S(2)}) %collective-permute-start.2) | collective-permute-done | bytes 1179680 | tf_op jit(solution)/shard_map/ppermute | solution.py:94
  74.6 4.7 copy.216
  79.4 4.8 copy.187
  84.2 4.5 fusion.54
  91.9 9.4 %bitcast_subtract_fusion = (f32[16,4,128,64]{3,0,1,2:T(8,128)}, f32[16,4,128,64]{3,0,1,2:T(8,128)}) fusion(f32[16,128,4,64]{3,2,1,0:T(4,128)} %reshape.302), kind=kOutput, calls=%fused_computation.42 | output fusion | flops 67108864 | bytes 6291456 | tf_op jit(solution)/shard_map/jit(cumsum)/reduce_window_sum | solution.py:33
  101.3 4.8 copy.196
  118.8 5.7 %convolution_convert_fusion.2 = bf16[2048,256]{1,0:T(8,128)(2,1)} fusion(bf16[2048,1152]{1,0:T(8,128)(2,1)} %bitcast.152, bf16[1152,256]{1,0:T(8,128)(2,1)} %param.19), kind=kOutput, calls=%fused_computation.66 | convolution fusion | flops 1208483840 | bytes 6356992 | tf_op jit(solution)/shard_map/dot_general | solution.py:108
  128.3 22.3 %fusion.1 = f32[16,4,8,16,128]{4,3,2,1,0:T(8,128)S(1)} fusion(f32[16,4,128,64]{2,3,1,0:T(8,128)} %copy.196, f32[16,4,8,64]{3,2,1,0:T(8,128)S(1)} %copy.191, f32[16,4,128,64]{2,3,1,0:T(8,128)S(1)} %bitcast.135, pred[8,128]{1,0:T(8,128)(4,1)S(1)} %iota_compare_fusion.1, f32[16,4,8,16,64]{4,3,2,1,0:T(8,128)} %bitcast.161, f32[16,4,8,16,64]{4,0,1,3,2:T(8,128)} %bitcast.147), kind=kOutput, calls=%fused_computation.1 | convolution fusion | flops 818937856 | bytes 12715008 | tf_op jit(solution)/shard_map/nhbqc,nhbsc->nhbqs/dot_general | solution.py:46
  166.9 6.7 %all-to-all-start.3 = ((bf16[1,16,128,256]{3,1,0,2:T(8,128)(2,1)}), bf16[1,16,128,256]{3,1,0,2:T(8,128)(2,1)}, u32[]{:S(2)}, u32[]{:S(2)}) async-start(bf16[1,16,128,256]{3,1,0,2:T(8,128)(2,1)} %multiply_convert_fusion.1), calls=%async_computation.3 | async-start | bytes 2097152 | tf_op jit(solution)/shard_map/all_to_all | solution.py:137
  176.5 22.5 %all-to-all-done.3 = bf16[1,16,128,256]{3,1,0,2:T(8,128)(2,1)} async-done(((bf16[1,16,128,256]{3,1,0,2:T(8,128)(2,1)}), bf16[1,16,128,256]{3,1,0,2:T(8,128)(2,1)}, u32[]{:S(2)}, u32[]{:S(2)}) %all-to-all-start.3) | async-done | bytes 1048608 | tf_op jit(solution)/shard_map/all_to_all | solution.py:137
  204.8 23.8 %all-to-all-done.1 = bf16[1,16,128,256]{3,1,0,2:T(8,128)(2,1)} async-done(((bf16[1,16,128,256]{3,1,0,2:T(8,128)(2,1)}), bf16[1,16,128,256]{3,1,0,2:T(8,128)(2,1)}, u32[]{:S(2)}, u32[]{:S(2)}) %all-to-all-start.1) | async-done | bytes 1048608 | tf_op jit(solution)/shard_map/all_to_all | solution.py:136
  233.8 24.2 %all-to-all-done.2 = bf16[1,16,128,256]{3,1,0,2:T(8,128)(2,1)S(1)} async-done(((bf16[1,16,128,256]{3,1,0,2:T(8,128)(2,1)}), bf16[1,16,128,256]{3,1,0,2:T(8,128)(2,1)S(1)}, u32[]{:S(2)}, u32[]{:S(2)}) %all-to-all-start.2) | async-done | bytes 1048608 | tf_op jit(solution)/shard_map/all_to_all | solution.py:135
  271.0 4.6 copy.177
  275.6 7.5 %bitcast_subtract_fusion.1 = (f32[16,4,128,64]{3,0,1,2:T(8,128)}, f32[16,4,128,64]{3,0,1,2:T(8,128)}) fusion(f32[16,128,4,64]{3,0,2,1:T(8,128)} %copy.177), kind=kOutput, calls=%fused_computation.45 | output fusion | flops 67108864 | bytes 6291456 | tf_op jit(solution)/shard_map/jit(cumsum)/reduce_window_sum | solution.py:33
  283.1 4.8 copy.185
  299.8 22.4 %fusion.6 = f32[16,4,8,16,128]{4,3,2,1,0:T(8,128)S(1)} fusion(f32[16,4,128,64]{2,3,1,0:T(8,128)} %copy.185, f32[16,4,8,64]{3,2,1,0:T(8,128)S(1)} %copy.178, f32[16,4,128,64]{2,3,1,0:T(8,128)} %bitcast.140, pred[8,128]{1,0:T(8,128)(4,1)S(1)} %iota_compare_fusion.1, f32[16,4,8,16,64]{4,3,2,1,0:T(8,128)} %bitcast.160, f32[16,4,8,16,64]{4,0,1,3,2:T(8,128)} %bitcast.145), kind=kOutput, calls=%fused_computation.6 | convolution fusion | flops 818937856 | bytes 12715008 | tf_op jit(solution)/shard_map/nhbqc,nhbsc->nhbqs/dot_general | solution.py:46
  338.3 30.6 %all_to_all.69 = bf16[1,128,16,256]{3,2,0,1:T(8,128)(2,1)S(1)} all-to-all(bf16[1,128,16,256]{3,2,0,1:T(8,128)(2,1)S(1)} %fusion.68), channel_id=1, replica_groups=mesh['seq'=8,'mp'=4] {'seq'}, dimensions={1} | all-to-all | bytes 2097152 | tf_op jit(solution)/shard_map/all_to_all | solution.py:158
  373.8 91.0 %all-reduce.2.cloned.1.call-done = bf16[1,16,128,1152]{3,2,1,0:T(8,128)(2,1)} async-done(((bf16[1,16,128,1152]{3,2,1,0:T(8,128)(2,1)}), bf16[1,16,128,1152]{3,2,1,0:T(8,128)(2,1)}) %all-reduce.2.cloned.1.call-update) | async-done | bytes 4718608 | tf_op jit(solution)/shard_map/psum | solution.py:166
  464.8 5.3 convert_reduce_fusion.1
  475.5 8.2 %all-gather.3.cloned.1.call-done = bf16[1152,1152]{1,0:T(8,128)(2,1)} async-done(((bf16[144,1152]{1,0:T(8,128)(2,1)}), bf16[1152,1152]{1,0:T(8,128)(2,1)}) %all-gather.3.cloned.1.call-update) | async-done | bytes 2654224 | tf_op jit(solution)/shard_map/all_gather | solution.py:175
  483.7 18.4 %convolution_convert_fusion = bf16[2048,1152]{1,0:T(8,128)(2,1)} fusion(bf16[1152,1152]{0,1:T(8,128)(2,1)} %all-gather.5.cloned.1.call-done, bf16[2048,1152]{1,0:T(8,128)(2,1)} %bitcast.153, bf16[1152,1152]{1,0:T(8,128)(2,1)} %all-gather.3.cloned.1.call-done), kind=kOutput, calls=%fused_computation.40 | convolution fusion | flops 10881073152 | bytes 14745600 | tf_op jit(solution)/shard_map/dot_general | solution.py:180
  502.1 46.6 %reduce-scatter.2.cloned.1.call-done = bf16[1,16,32,1152]{3,2,1,0:T(8,128)(2,1)} async-done(((bf16[1,16,128,1152]{3,2,1,0:T(8,128)(2,1)}), bf16[1,16,32,1152]{3,2,1,0:T(8,128)(2,1)}) %reduce-scatter.2.cloned.1.call-update) | async-done | bytes 1179664 | tf_op jit(solution)/shard_map/reduce_scatter | solution.py:187
  (144 shorter events, 123.9 us)
Async XLA Ops:
  7.4 361.6 %copy-start = (bf16[256,1152]{1,0:T(8,128)(2,1)S(1)}, bf16[256,1152]{1,0:T(8,128)(2,1)}, u32[]{:S(2)}) copy-start(bf16[256,1152]{1,0:T(8,128)(2,1)} %param.26) | copy-start | bytes 1769476
  7.4 51.3 %copy-start.7 = (bf16[1,16,32,1152]{3,2,1,0:T(8,128)(2,1)S(1)}, bf16[1,16,32,1152]{3,2,1,0:T(8,128)(2,1)}, u32[]{:S(2)}) copy-start(bf16[1,16,32,1152]{3,2,1,0:T(8,128)(2,1)} %param.15) | copy-start | bytes 3538948
  7.4 16.5 %collective-permute-start = (bf16[1,16,32,1152]{3,2,1,0:T(8,128)(2,1)}, bf16[1,16,32,1152]{3,2,1,0:T(8,128)(2,1)S(1)}, u32[]{:S(2)}, u32[]{:S(2)}) collective-permute-start(bf16[1,16,32,1152]{3,2,1,0:T(8,128)(2,1)} %param.15), channel_id=1, source_target_pairs={{0,1},{1,2},{2,3},{3,0},{4,5},{5,6},{6,7},{7,4},{8,9},{9,10},{10,1... | collective-permute-start | bytes 3538952 | tf_op jit(solution)/shard_map/ppermute | solution.py:94
  23.9 15.7 %collective-permute-start.1 = (bf16[1,16,32,1152]{3,2,1,0:T(8,128)(2,1)S(1)}, bf16[1,16,32,1152]{3,2,1,0:T(8,128)(2,1)}, u32[]{:S(2)}, u32[]{:S(2)}) collective-permute-start(bf16[1,16,32,1152]{3,2,1,0:T(8,128)(2,1)S(1)} %collective-permute-done), channel_id=1, source_target_pairs={{0,1},{1,2},{2,3},{3,0},{4,5},{5,6},{6,7},{7,4},{8,9},{9,10},{10,1... | collective-permute-start | bytes 3538952 | tf_op jit(solution)/shard_map/ppermute | solution.py:94
  39.6 15.9 %collective-permute-start.2 = (bf16[1,16,32,1152]{3,2,1,0:T(8,128)(2,1)}, bf16[1,16,32,1152]{3,2,1,0:T(8,128)(2,1)}, u32[]{:S(2)}, u32[]{:S(2)}) collective-permute-start(bf16[1,16,32,1152]{3,2,1,0:T(8,128)(2,1)} %collective-permute-done.1), channel_id=1, source_target_pairs={{0,1},{1,2},{2,3},{3,0},{4,5},{5,6},{6,7},{7,4},{8,9},{9,10},{10,1... | collective-permute-start | bytes 3538952 | tf_op jit(solution)/shard_map/ppermute | solution.py:94
  71.5 7.9 %copy-start.9 = (bf16[2048,256]{1,0:T(8,128)(2,1)}, bf16[2048,256]{1,0:T(8,128)(2,1)S(1)}, u32[]{:S(2)}) copy-start(bf16[2048,256]{1,0:T(8,128)(2,1)S(1)} %convolution_convert_fusion.4) | copy-start | bytes 3145732
  79.4 4.8 copy-start.24
  88.7 12.6 %copy-start.11 = (bf16[2048,256]{1,0:T(8,128)(2,1)}, bf16[2048,256]{1,0:T(8,128)(2,1)S(1)}, u32[]{:S(2)}) copy-start(bf16[2048,256]{1,0:T(8,128)(2,1)S(1)} %fusion.54) | copy-start | bytes 3145732
  101.3 5.9 %copy-start.21 = (bf16[1152,256]{1,0:T(8,128)(2,1)S(1)}, bf16[1152,256]{1,0:T(8,128)(2,1)}, u32[]{:S(2)}) copy-start(bf16[1152,256]{1,0:T(8,128)(2,1)} %param.18) | copy-start | bytes 1769476
  118.7 9.5 %copy-start.6 = (f32[16,128,4,64]{1,3,2,0:T(8,128)}, f32[16,128,4,64]{1,3,2,0:T(8,128)S(1)}, u32[]{:S(2)}) copy-start(f32[16,128,4,64]{1,3,2,0:T(8,128)S(1)} %copy.194) | copy-start | bytes 6291460
  128.2 22.4 %copy-start.3 = (bf16[32,8,16,128]{3,2,1,0:T(8,128)(2,1)}, bf16[32,8,16,128]{3,2,1,0:T(8,128)(2,1)S(1)}, u32[]{:S(2)}) copy-start(bf16[32,8,16,128]{3,2,1,0:T(8,128)(2,1)S(1)} %copy.223) | copy-start | bytes 3145732
  166.9 36.4 %copy-start.13 = (bf16[2048,256]{1,0:T(8,128)(2,1)S(1)}, bf16[2048,256]{1,0:T(8,128)(2,1)}, u32[]{:S(2)}) copy-start(bf16[2048,256]{1,0:T(8,128)(2,1)} %copy-done.12) | copy-start | bytes 3145732
  166.9 32.1 %all-to-all-start.3 = ((bf16[1,16,128,256]{3,1,0,2:T(8,128)(2,1)}), bf16[1,16,128,256]{3,1,0,2:T(8,128)(2,1)}, u32[]{:S(2)}, u32[]{:S(2)}) async-start(bf16[1,16,128,256]{3,1,0,2:T(8,128)(2,1)} %multiply_convert_fusion.1), calls=%async_computation.3 | async-start | bytes 2097152 | tf_op jit(solution)/shard_map/all_to_all | solution.py:137
  173.7 58.6 %copy-start.10 = (bf16[2048,256]{1,0:T(8,128)(2,1)S(1)}, bf16[2048,256]{1,0:T(8,128)(2,1)}, u32[]{:S(2)}) copy-start(bf16[2048,256]{1,0:T(8,128)(2,1)} %copy-done.9) | copy-start | bytes 3145732
  199.0 29.6 %all-to-all-start.1 = ((bf16[1,16,128,256]{3,1,0,2:T(8,128)(2,1)}), bf16[1,16,128,256]{3,1,0,2:T(8,128)(2,1)}, u32[]{:S(2)}, u32[]{:S(2)}) async-start(bf16[1,16,128,256]{3,1,0,2:T(8,128)(2,1)} %copy.173), calls=%async_computation.1 | async-start | bytes 2097152 | tf_op jit(solution)/shard_map/all_to_all | solution.py:136
  228.7 29.3 %all-to-all-start.2 = ((bf16[1,16,128,256]{3,1,0,2:T(8,128)(2,1)}), bf16[1,16,128,256]{3,1,0,2:T(8,128)(2,1)S(1)}, u32[]{:S(2)}, u32[]{:S(2)}) async-start(bf16[1,16,128,256]{3,1,0,2:T(8,128)(2,1)} %copy.180), calls=%async_computation.2 | async-start | bytes 2097152 | tf_op jit(solution)/shard_map/all_to_all | solution.py:135
  258.0 7.7 %copy-start.14 = (bf16[1,16,128,256]{3,1,0,2:T(8,128)(2,1)}, bf16[1,16,128,256]{3,1,0,2:T(8,128)(2,1)S(1)}, u32[]{:S(2)}) copy-start(bf16[1,16,128,256]{3,1,0,2:T(8,128)(2,1)S(1)} %all-to-all-done.2) | copy-start | bytes 3145732
  258.0 33.8 %all-to-all-start = ((bf16[1,16,128,256]{3,1,0,2:T(8,128)(2,1)}), bf16[1,16,128,256]{3,1,0,2:T(8,128)(2,1)}, u32[]{:S(2)}, u32[]{:S(2)}) async-start(bf16[1,16,128,256]{3,1,0,2:T(8,128)(2,1)} %copy.168), calls=%async_computation | async-start | bytes 2097152 | tf_op jit(solution)/shard_map/all_to_all | solution.py:134
  262.3 202.6 %all-reduce.2.cloned.1.call-start = ((), (), s32[]{:S(2)}) async-start(), calls=%async_computation.6 | async-start | bytes 9437184 | tf_op jit(solution)/shard_map/psum | solution.py:166
  283.1 6.0 %copy-start.15 = (bf16[1,16,128,256]{3,1,0,2:T(8,128)(2,1)S(1)}, bf16[1,16,128,256]{3,1,0,2:T(8,128)(2,1)}, u32[]{:S(2)}) copy-start(bf16[1,16,128,256]{3,1,0,2:T(8,128)(2,1)} %copy-done.14) | copy-start | bytes 3145732
  299.8 22.4 %copy-start.5 = (bf16[1,16,128,256]{2,3,1,0:T(8,128)(2,1)S(1)}, bf16[1,16,128,256]{2,3,1,0:T(8,128)(2,1)}, u32[]{:S(2)}) copy-start(bf16[1,16,128,256]{2,3,1,0:T(8,128)(2,1)} %copy.204) | copy-start | bytes 3145732
  372.6 102.8 %all-gather.5.cloned.1.call-start = ((), (), s32[]{:S(2)}) async-start(), calls=%async_computation.8 | async-start | bytes 2985984 | tf_op jit(solution)/shard_map/all_gather | solution.py:182
  373.2 110.5 %all-gather.3.cloned.1.call-start = ((), (), s32[]{:S(2)}) async-start(), calls=%async_computation.7 | async-start | bytes 2985984 | tf_op jit(solution)/shard_map/all_gather | solution.py:175
  373.8 174.9 %reduce-scatter.2.cloned.1.call-start = ((), (), s32[]{:S(2)}) async-start(), calls=%async_computation.9 | async-start | bytes 5898240 | tf_op jit(solution)/shard_map/reduce_scatter | solution.py:187
  (12 other events, 38.0 us)
Sparse Core Ops, SparseCore 0:
  372.7 92.0 all-reduce.1
  502.2 46.4 reduce-scatter.1
Sparse Core Ops, SparseCore 1:
  375.3 52.9 all-gather.4
  430.3 53.4 all-gather.2
